TPU v7x, 128 devices: a whole 4x4x4 slice. The times are simulated.
128 devices in a mesh: shot: 4 (over y_lo, core), gx: 4 (over z), gy: 8 (over x, y_hi).
Axes of the slice: x: 4, y: 4 (y_hi: 2, y_lo: 2; y = y_hi * 2 + y_lo), z: 4, core: 2. Of those that a mesh axis runs over, the one named last changes fastest.
Arguments:
- model_tiles: float32 [256, 256, 128], P(('shot', 'gx'), 'gy'), may hold values from 0.2 to 0.45
- owner_map: int32 [16], replicated, may hold values from 0 to 15, each once
- offsets: int32 [4], P('shot'), may hold values from 0 to 12
- field_now: float32 [4, 2, 64, 256, 128], P('shot', None, 'gx', 'gy'), may hold values from -6 to 6
- field_prev: float32 [4, 2, 64, 256, 128], P('shot', None, 'gx', 'gy'), may hold values from -6 to 6
- sources: int32 [4, 2, 3], P('shot'), may hold values from 0 to 255, as said below
- wavelet: float32 [4, 2, 8], P('shot'), may hold values from -6 to 6
- receivers: int32 [4, 256, 3], P('shot'), may hold values from 0 to 255, as said below
Outputs:
- out_now: float32 [4, 2, 64, 256, 128], P('shot', None, 'gx', 'gy')
- out_prev: float32 [4, 2, 64, 256, 128], P('shot', None, 'gx', 'gy')
- traces: float32 [4, 2, 256, 8], P('shot')
Inputs may be any that keep to these rules, and one draw needn't show every extreme that they name: `sources`: each row is a cell of the group's aperture: first entry below 64, second below 256, third below 128. `receivers`: each row is a cell of the group's aperture: first entry below 64, second below 256, third below 128.
All inputs are finite; a program needn't handle non-finite values.
Results may differ from a plain program's by a relative error of at most 0.0003.
Values sent between devices are 32-bit elements; how exact they have to be, the bound alone decides.
A program may use at most 128 MiB of HBM per device.

v0:
```python
import jax
import jax.numpy as jnp
from jax import lax
from jax.sharding import PartitionSpec as P

STEPS = 8
center_weight = -2.5
near_weight = 4.0 / 3.0
far_weight = -1.0 / 12.0
damp_peak = 0.3


def extended_2(cells, sides, width):
    for axis, dim in sides:
        count = lax.axis_size(axis)
        ends = count - 1
        head = lax.slice_in_dim(cells, 0, width, axis=dim)
        tail = lax.slice_in_dim(cells, cells.shape[dim] - width, cells.shape[dim], axis=dim)
        cells = jnp.concatenate(
            [
                lax.ppermute(tail, axis, [(i, (i + 1) % count) for i in range(ends)]),
                cells,
                lax.ppermute(head, axis, [((i + 1) % count, i) for i in range(ends)]),
            ],
            axis=dim,
        )
    return cells


def depth_ahead(field, reach):
    filler = jnp.zeros(field.shape[:-1] + (reach,), field.dtype)
    return jnp.concatenate([field[..., reach:], filler], axis=-1)


def depth_behind(field, reach):
    filler = jnp.zeros(field.shape[:-1] + (reach,), field.dtype)
    return jnp.concatenate([filler, field[..., :-reach]], axis=-1)


def laplace(extended):
    middle = extended[:, 2:-2, 2:-2]
    along_x = (
        center_weight * middle
        + near_weight * (extended[:, 3:-1, 2:-2] + extended[:, 1:-3, 2:-2])
        + far_weight * (extended[:, 4:, 2:-2] + extended[:, :-4, 2:-2])
    )
    along_y = (
        center_weight * middle
        + near_weight * (extended[:, 2:-2, 3:-1] + extended[:, 2:-2, 1:-3])
        + far_weight * (extended[:, 2:-2, 4:] + extended[:, 2:-2, :-4])
    )
    along_z = (
        center_weight * middle
        + near_weight * (depth_ahead(middle, 1) + depth_behind(middle, 1))
        + far_weight * (depth_ahead(middle, 2) + depth_behind(middle, 2))
    )
    return along_x + along_y + along_z


def damping(x_cells, y_cells, width, x_total, y_total):
    x_depth = (
        jnp.maximum(width - jnp.minimum(x_cells + 1, x_total - x_cells), 0).astype(jnp.float32)
        / width
    )
    y_depth = (
        jnp.maximum(width - jnp.minimum(y_cells + 1, y_total - y_cells), 0).astype(jnp.float32)
        / width
    )
    return damp_peak * (x_depth[:, None] * x_depth[:, None] + y_depth[None, :] * y_depth[None, :])


def injection(x_cells, y_cells, z_cells, source_cells, amplitude):
    on_x = (x_cells[None, :] == source_cells[:, 0:1]).astype(jnp.float32)
    on_y = (y_cells[None, :] == source_cells[:, 1:2]).astype(jnp.float32)
    on_z = (z_cells[None, :] == source_cells[:, 2:3]).astype(jnp.float32)
    return (
        amplitude[:, None, None, None]
        * on_x[:, :, None, None]
        * on_y[:, None, :, None]
        * on_z[:, None, None, :]
    )


def advance(extended, previous, coef, damp, inject):
    middle = extended[:, 2:-2, 2:-2]
    return (2.0 * middle - (1.0 - damp) * previous + coef * laplace(extended) + inject) / (
        1.0 + damp
    )


def sample(field, receiver_cells, x_start, y_start):
    size_x, size_y = (field.shape[1], field.shape[2])
    local_x = receiver_cells[:, 0] - x_start
    local_y = receiver_cells[:, 1] - y_start
    inside = (local_x >= 0) & (local_x < size_x) & (local_y >= 0) & (local_y < size_y)
    values = field[
        :, jnp.clip(local_x, 0, size_x - 1), jnp.clip(local_y, 0, size_y - 1), receiver_cells[:, 2]
    ]
    return jnp.where(inside[None, :], values, 0.0)


def local(model_tiles, owner_map, offsets, field_now, field_prev, sources, wavelet, receivers):
    block_x, block_y, depth = model_tiles.shape
    column_index = lax.axis_index("gx")
    row_index = lax.axis_index("gy")
    across = lax.axis_size("gx")
    total_x = block_x * across
    total_y = block_y * lax.axis_size("gy")
    shift_x = offsets[0]
    tile_total = owner_map.shape[0]
    column_ids = jnp.arange(tile_total, dtype=jnp.int32)
    wanted = jnp.sum(jnp.where(column_ids == shift_x + column_index, owner_map, 0))
    piece = lax.all_gather(model_tiles, ("shot", "gx"), axis=0, tiled=True)
    rows = wanted * block_x + jnp.arange(block_x, dtype=jnp.int32)
    inside = (rows >= 0) & (rows < piece.shape[0])
    taken = jnp.take(piece, jnp.clip(rows, 0, piece.shape[0] - 1), axis=0)
    speed = jnp.where(inside[:, None, None], taken, jnp.zeros_like(model_tiles))
    coef = speed * speed
    current = field_now[0]
    previous = field_prev[0]
    source_cells = sources[0]
    amplitudes = wavelet[0]
    receiver_cells = receivers[0]
    x_start = column_index * block_x
    y_start = row_index * block_y
    x_here = x_start + jnp.arange(block_x, dtype=jnp.int32)
    y_here = y_start + jnp.arange(block_y, dtype=jnp.int32)
    z_cells = jnp.arange(depth, dtype=jnp.int32)
    damp = damping(x_here, y_here, block_x, total_x, total_y)[:, :, None]
    recorded = []
    for step in range(STEPS):
        extended = extended_2(current, (("gx", 1), ("gy", 2)), 2)
        inject = injection(x_here, y_here, z_cells, source_cells, amplitudes[:, step])
        fresh = advance(extended, previous, coef, damp, inject)
        recorded.append(sample(fresh, receiver_cells, x_start, y_start))
        previous = current
        current = fresh
    traces = lax.psum(jnp.stack(recorded, axis=-1), ("gx", "gy"))
    return (current[None], previous[None], traces[None])


def solution(mesh):
    return jax.shard_map(
        local,
        mesh=mesh,
        in_specs=(
            P(("shot", "gx"), "gy", None),
            P(),
            P("shot"),
            P("shot", None, "gx", "gy", None),
            P("shot", None, "gx", "gy", None),
            P("shot", None, None),
            P("shot", None, None),
            P("shot", None, None),
        ),
        out_specs=(
            P("shot", None, "gx", "gy", None),
            P("shot", None, "gx", "gy", None),
            P("shot", None, None, None),
        ),
        check_vma=False,
    )
```

profile of v0, /device:TPU:0, one launch (start us, length us, event | category | flops | bytes accessed | tf_op | source)
XLA Modules:
  0.0 552.9 jit_solution(16876477504030605119)
XLA Ops:
  28.2 6.1 %collective-permute-start.3 = (f32[2,20,2,128]{3,2,1,0:T(2,128)S(1)}, f32[2,20,2,128]{3,2,1,0:T(2,128)S(1)}, u32[]{:S(2)}, u32[]{:S(2)}) collective-permute-start(f32[2,20,2,128]{3,2,1,0:T(2,128)S(1)} %get-tuple-element.57), channel_id=1, source_target_pairs={{0,1},{1,2},{2,3},{3,4},{4,5},{5,6},{6,7},{8,9},{9,10},{10,11},{11... | collective-permute-start | bytes 122888 | tf_op jit(solution)/shard_map/ppermute | solution.py:21
  37.5 24.6 %all-gather.2.cloned.1.call-done = f32[256,32,128]{2,1,0:T(8,128)} async-done(((f32[16,32,128]{2,1,0:T(8,128)}), f32[256,32,128]{2,1,0:T(8,128)}) %all-gather.2.cloned.1.call-update) | async-done | bytes 4194320 | tf_op jit(solution)/shard_map/all_gather | solution.py:113
  77.4 6.1 %collective-permute-start.7 = (f32[2,20,2,128]{3,2,1,0:T(2,128)S(1)}, f32[2,20,2,128]{3,2,1,0:T(2,128)S(1)}, u32[]{:S(2)}, u32[]{:S(2)}) collective-permute-start(f32[2,20,2,128]{3,2,1,0:T(2,128)S(1)} %get-tuple-element.53), channel_id=1, source_target_pairs={{0,1},{1,2},{2,3},{3,4},{4,5},{5,6},{6,7},{8,9},{9,10},{10,11},{11... | collective-permute-start | bytes 122888 | tf_op jit(solution)/shard_map/ppermute | solution.py:21
  84.4 16.7 %copy.515 = f32[2,16,32,128]{0,3,2,1:T(8,128)} copy(f32[2,16,32,128]{3,2,1,0:T(8,128)S(1)} %fusion.94) | data formatting | bytes 1048576 | tf_op jit(solution)/shard_map/div | solution.py:86
  107.5 5.0 collective-permute-start.9
  115.8 6.5 %collective-permute-start.11 = (f32[2,20,2,128]{3,2,1,0:T(2,128)S(1)}, f32[2,20,2,128]{3,2,1,0:T(2,128)S(1)}, u32[]{:S(2)}, u32[]{:S(2)}) collective-permute-start(f32[2,20,2,128]{3,2,1,0:T(2,128)S(1)} %get-tuple-element.49), channel_id=1, source_target_pairs={{0,1},{1,2},{2,3},{3,4},{4,5},{5,6},{6,7},{8,9},{9,10},{10,11},{11... | collective-permute-start | bytes 122888 | tf_op jit(solution)/shard_map/ppermute | solution.py:21
  123.2 16.7 %copy.516 = f32[2,16,32,128]{0,3,2,1:T(8,128)} copy(f32[2,16,32,128]{3,2,1,0:T(8,128)S(1)} %fusion.82) | data formatting | bytes 1048576 | tf_op jit(solution)/shard_map/div | solution.py:86
  146.4 4.9 collective-permute-start.13
  154.5 6.9 %collective-permute-start.15 = (f32[2,20,2,128]{3,2,1,0:T(2,128)S(1)}, f32[2,20,2,128]{3,2,1,0:T(2,128)S(1)}, u32[]{:S(2)}, u32[]{:S(2)}) collective-permute-start(f32[2,20,2,128]{3,2,1,0:T(2,128)S(1)} %get-tuple-element.45), channel_id=1, source_target_pairs={{0,1},{1,2},{2,3},{3,4},{4,5},{5,6},{6,7},{8,9},{9,10},{10,11},{11... | collective-permute-start | bytes 122888 | tf_op jit(solution)/shard_map/ppermute | solution.py:21
  162.4 16.7 %copy.517 = f32[2,16,32,128]{0,3,2,1:T(8,128)} copy(f32[2,16,32,128]{3,2,1,0:T(8,128)S(1)} %fusion.70) | data formatting | bytes 1048576 | tf_op jit(solution)/shard_map/div | solution.py:86
  185.6 4.9 collective-permute-start.17
  193.7 7.1 %collective-permute-start.19 = (f32[2,20,2,128]{3,2,1,0:T(2,128)S(1)}, f32[2,20,2,128]{3,2,1,0:T(2,128)S(1)}, u32[]{:S(2)}, u32[]{:S(2)}) collective-permute-start(f32[2,20,2,128]{3,2,1,0:T(2,128)S(1)} %get-tuple-element.41), channel_id=1, source_target_pairs={{0,1},{1,2},{2,3},{3,4},{4,5},{5,6},{6,7},{8,9},{9,10},{10,11},{11... | collective-permute-start | bytes 122888 | tf_op jit(solution)/shard_map/ppermute | solution.py:21
  201.7 16.7 %copy.518 = f32[2,16,32,128]{0,3,2,1:T(8,128)} copy(f32[2,16,32,128]{3,2,1,0:T(8,128)S(1)} %fusion.58) | data formatting | bytes 1048576 | tf_op jit(solution)/shard_map/div | solution.py:86
  224.9 4.9 collective-permute-start.21
  233.0 6.9 %collective-permute-start.23 = (f32[2,20,2,128]{3,2,1,0:T(2,128)S(1)}, f32[2,20,2,128]{3,2,1,0:T(2,128)S(1)}, u32[]{:S(2)}, u32[]{:S(2)}) collective-permute-start(f32[2,20,2,128]{3,2,1,0:T(2,128)S(1)} %get-tuple-element.37), channel_id=1, source_target_pairs={{0,1},{1,2},{2,3},{3,4},{4,5},{5,6},{6,7},{8,9},{9,10},{10,11},{11... | collective-permute-start | bytes 122888 | tf_op jit(solution)/shard_map/ppermute | solution.py:21
  240.9 16.7 %copy.519 = f32[2,16,32,128]{0,3,2,1:T(8,128)} copy(f32[2,16,32,128]{3,2,1,0:T(8,128)S(1)} %fusion.46) | data formatting | bytes 1048576 | tf_op jit(solution)/shard_map/div | solution.py:86
  264.1 4.9 collective-permute-start.25
  272.2 6.9 %collective-permute-start.27 = (f32[2,20,2,128]{3,2,1,0:T(2,128)S(1)}, f32[2,20,2,128]{3,2,1,0:T(2,128)S(1)}, u32[]{:S(2)}, u32[]{:S(2)}) collective-permute-start(f32[2,20,2,128]{3,2,1,0:T(2,128)S(1)} %get-tuple-element.33), channel_id=1, source_target_pairs={{0,1},{1,2},{2,3},{3,4},{4,5},{5,6},{6,7},{8,9},{9,10},{10,11},{11... | collective-permute-start | bytes 122888 | tf_op jit(solution)/shard_map/ppermute | solution.py:21
  280.1 16.7 %copy.520 = f32[2,16,32,128]{0,3,2,1:T(8,128)} copy(f32[2,16,32,128]{3,2,1,0:T(8,128)S(1)} %fusion.34) | data formatting | bytes 1048576 | tf_op jit(solution)/shard_map/div | solution.py:86
  303.2 4.9 collective-permute-start.29
  311.3 7.2 %collective-permute-start.31 = (f32[2,20,2,128]{3,2,1,0:T(2,128)S(1)}, f32[2,20,2,128]{3,2,1,0:T(2,128)S(1)}, u32[]{:S(2)}, u32[]{:S(2)}) collective-permute-start(f32[2,20,2,128]{3,2,1,0:T(2,128)S(1)} %get-tuple-element.29), channel_id=1, source_target_pairs={{0,1},{1,2},{2,3},{3,4},{4,5},{5,6},{6,7},{8,9},{9,10},{10,11},{11... | collective-permute-start | bytes 122888 | tf_op jit(solution)/shard_map/ppermute | solution.py:21
  319.5 16.7 %copy.521 = f32[2,16,32,128]{0,3,2,1:T(8,128)} copy(f32[2,16,32,128]{3,2,1,0:T(8,128)S(1)} %fusion.22) | data formatting | bytes 1048576 | tf_op jit(solution)/shard_map/div | solution.py:86
  341.3 16.8 %copy.522 = f32[2,16,32,128]{0,3,2,1:T(8,128)} copy(f32[2,16,32,128]{3,2,1,0:T(8,128)S(1)} %fusion.10) | data formatting | bytes 1048576 | tf_op jit(solution)/shard_map/div | solution.py:86
  362.6 183.4 %psum.7 = f32[1,2,256,8]{2,3,1,0:T(8,128)} all-reduce(f32[1,2,256,8]{2,3,1,0:T(8,128)S(1)} %bitcast.70), channel_id=1, replica_groups=mesh['shot'=4,'gx'=4,'gy'=8] {'gx','gy'}, use_global_device_ids=true, to_apply=%region_1.2 | all-reduce | flops 4096 | bytes 32768 | tf_op jit(solution)/shard_map/psum | solution.py:138
  (164 shorter events, 112.2 us)
Async XLA Ops:
  7.2 54.9 %all-gather.2.cloned.1.call-start = ((), (), s32[]{:S(2)}) async-start(), calls=%async_computation | async-start | bytes 4456448 | tf_op jit(solution)/shard_map/all_gather | solution.py:113
  8.8 17.0 %collective-permute-start = (f32[2,2,32,128]{3,2,1,0:T(8,128)S(1)}, f32[2,2,32,128]{3,2,1,0:T(8,128)S(1)}, u32[]{:S(2)}, u32[]{:S(2)}) collective-permute-start(f32[2,2,32,128]{3,2,1,0:T(8,128)S(1)} %get-tuple-element.104), channel_id=1, source_target_pairs={{8,0},{16,8},{24,16},{9,1},{17,9},{25,17},{10,2},{18,10},{26,18},{... | collective-permute-start | bytes 196616 | tf_op jit(solution)/shard_map/ppermute | solution.py:23
  10.1 15.8 %collective-permute-start.1 = (f32[2,2,32,128]{3,2,1,0:T(8,128)S(1)}, f32[2,2,32,128]{3,2,1,0:T(8,128)S(1)}, u32[]{:S(2)}, u32[]{:S(2)}) collective-permute-start(f32[2,2,32,128]{3,2,1,0:T(8,128)S(1)} %get-tuple-element.105), channel_id=1, source_target_pairs={{0,8},{8,16},{16,24},{1,9},{9,17},{17,25},{2,10},{10,18},{18,26},{... | collective-permute-start | bytes 196616 | tf_op jit(solution)/shard_map/ppermute | solution.py:21
  26.9 7.7 %collective-permute-start.2 = (f32[2,20,2,128]{3,2,1,0:T(2,128)S(1)}, f32[2,20,2,128]{3,2,1,0:T(2,128)S(1)}, u32[]{:S(2)}, u32[]{:S(2)}) collective-permute-start(f32[2,20,2,128]{3,2,1,0:T(2,128)S(1)} %get-tuple-element.56), channel_id=1, source_target_pairs={{1,0},{2,1},{3,2},{4,3},{5,4},{6,5},{7,6},{9,8},{10,9},{11,10},{12... | collective-permute-start | bytes 122888 | tf_op jit(solution)/shard_map/ppermute | solution.py:23
  28.2 7.9 %collective-permute-start.3 = (f32[2,20,2,128]{3,2,1,0:T(2,128)S(1)}, f32[2,20,2,128]{3,2,1,0:T(2,128)S(1)}, u32[]{:S(2)}, u32[]{:S(2)}) collective-permute-start(f32[2,20,2,128]{3,2,1,0:T(2,128)S(1)} %get-tuple-element.57), channel_id=1, source_target_pairs={{0,1},{1,2},{2,3},{3,4},{4,5},{5,6},{6,7},{8,9},{9,10},{10,11},{11... | collective-permute-start | bytes 122888 | tf_op jit(solution)/shard_map/ppermute | solution.py:21
  68.1 6.8 %collective-permute-start.4 = (f32[2,2,32,128]{3,2,1,0:T(8,128)S(1)}, f32[2,2,32,128]{3,2,1,0:T(8,128)S(1)}, u32[]{:S(2)}, u32[]{:S(2)}) collective-permute-start(f32[2,2,32,128]{3,2,1,0:T(8,128)S(1)} %get-tuple-element.98), channel_id=1, source_target_pairs={{8,0},{16,8},{24,16},{9,1},{17,9},{25,17},{10,2},{18,10},{26,18},{... | collective-permute-start | bytes 196616 | tf_op jit(solution)/shard_map/ppermute | solution.py:23
  76.1 28.0 %collective-permute-start.6 = (f32[2,20,2,128]{3,2,1,0:T(2,128)S(1)}, f32[2,20,2,128]{3,2,1,0:T(2,128)S(1)}, u32[]{:S(2)}, u32[]{:S(2)}) collective-permute-start(f32[2,20,2,128]{3,2,1,0:T(2,128)S(1)} %get-tuple-element.52), channel_id=1, source_target_pairs={{1,0},{2,1},{3,2},{4,3},{5,4},{6,5},{7,6},{9,8},{10,9},{11,10},{12... | collective-permute-start | bytes 122888 | tf_op jit(solution)/shard_map/ppermute | solution.py:23
  77.4 26.7 %collective-permute-start.7 = (f32[2,20,2,128]{3,2,1,0:T(2,128)S(1)}, f32[2,20,2,128]{3,2,1,0:T(2,128)S(1)}, u32[]{:S(2)}, u32[]{:S(2)}) collective-permute-start(f32[2,20,2,128]{3,2,1,0:T(2,128)S(1)} %get-tuple-element.53), channel_id=1, source_target_pairs={{0,1},{1,2},{2,3},{3,4},{4,5},{5,6},{6,7},{8,9},{9,10},{10,11},{11... | collective-permute-start | bytes 122888 | tf_op jit(solution)/shard_map/ppermute | solution.py:21
  107.5 6.9 %collective-permute-start.9 = (f32[2,2,32,128]{3,2,1,0:T(8,128)S(1)}, f32[2,2,32,128]{3,2,1,0:T(8,128)S(1)}, u32[]{:S(2)}, u32[]{:S(2)}) collective-permute-start(f32[2,2,32,128]{3,2,1,0:T(8,128)S(1)} %get-tuple-element.93), channel_id=1, source_target_pairs={{0,8},{8,16},{16,24},{1,9},{9,17},{17,25},{2,10},{10,18},{18,26},{... | collective-permute-start | bytes 196616 | tf_op jit(solution)/shard_map/ppermute | solution.py:21
  114.5 28.5 %collective-permute-start.10 = (f32[2,20,2,128]{3,2,1,0:T(2,128)S(1)}, f32[2,20,2,128]{3,2,1,0:T(2,128)S(1)}, u32[]{:S(2)}, u32[]{:S(2)}) collective-permute-start(f32[2,20,2,128]{3,2,1,0:T(2,128)S(1)} %get-tuple-element.48), channel_id=1, source_target_pairs={{1,0},{2,1},{3,2},{4,3},{5,4},{6,5},{7,6},{9,8},{10,9},{11,10},{12... | collective-permute-start | bytes 122888 | tf_op jit(solution)/shard_map/ppermute | solution.py:23
  115.8 27.2 %collective-permute-start.11 = (f32[2,20,2,128]{3,2,1,0:T(2,128)S(1)}, f32[2,20,2,128]{3,2,1,0:T(2,128)S(1)}, u32[]{:S(2)}, u32[]{:S(2)}) collective-permute-start(f32[2,20,2,128]{3,2,1,0:T(2,128)S(1)} %get-tuple-element.49), channel_id=1, source_target_pairs={{0,1},{1,2},{2,3},{3,4},{4,5},{5,6},{6,7},{8,9},{9,10},{10,11},{11... | collective-permute-start | bytes 122888 | tf_op jit(solution)/shard_map/ppermute | solution.py:21
  146.4 6.8 %collective-permute-start.13 = (f32[2,2,32,128]{3,2,1,0:T(8,128)S(1)}, f32[2,2,32,128]{3,2,1,0:T(8,128)S(1)}, u32[]{:S(2)}, u32[]{:S(2)}) collective-permute-start(f32[2,2,32,128]{3,2,1,0:T(8,128)S(1)} %get-tuple-element.87), channel_id=1, source_target_pairs={{0,8},{8,16},{16,24},{1,9},{9,17},{17,25},{2,10},{10,18},{18,26},{... | collective-permute-start | bytes 196616 | tf_op jit(solution)/shard_map/ppermute | solution.py:21
  153.2 28.9 %collective-permute-start.14 = (f32[2,20,2,128]{3,2,1,0:T(2,128)S(1)}, f32[2,20,2,128]{3,2,1,0:T(2,128)S(1)}, u32[]{:S(2)}, u32[]{:S(2)}) collective-permute-start(f32[2,20,2,128]{3,2,1,0:T(2,128)S(1)} %get-tuple-element.44), channel_id=1, source_target_pairs={{1,0},{2,1},{3,2},{4,3},{5,4},{6,5},{7,6},{9,8},{10,9},{11,10},{12... | collective-permute-start | bytes 122888 | tf_op jit(solution)/shard_map/ppermute | solution.py:23
  154.5 27.6 %collective-permute-start.15 = (f32[2,20,2,128]{3,2,1,0:T(2,128)S(1)}, f32[2,20,2,128]{3,2,1,0:T(2,128)S(1)}, u32[]{:S(2)}, u32[]{:S(2)}) collective-permute-start(f32[2,20,2,128]{3,2,1,0:T(2,128)S(1)} %get-tuple-element.45), channel_id=1, source_target_pairs={{0,1},{1,2},{2,3},{3,4},{4,5},{5,6},{6,7},{8,9},{9,10},{10,11},{11... | collective-permute-start | bytes 122888 | tf_op jit(solution)/shard_map/ppermute | solution.py:21
  185.6 6.8 %collective-permute-start.17 = (f32[2,2,32,128]{3,2,1,0:T(8,128)S(1)}, f32[2,2,32,128]{3,2,1,0:T(8,128)S(1)}, u32[]{:S(2)}, u32[]{:S(2)}) collective-permute-start(f32[2,2,32,128]{3,2,1,0:T(8,128)S(1)} %get-tuple-element.81), channel_id=1, source_target_pairs={{0,8},{8,16},{16,24},{1,9},{9,17},{17,25},{2,10},{10,18},{18,26},{... | collective-permute-start | bytes 196616 | tf_op jit(solution)/shard_map/ppermute | solution.py:21
  192.4 29.1 %collective-permute-start.18 = (f32[2,20,2,128]{3,2,1,0:T(2,128)S(1)}, f32[2,20,2,128]{3,2,1,0:T(2,128)S(1)}, u32[]{:S(2)}, u32[]{:S(2)}) collective-permute-start(f32[2,20,2,128]{3,2,1,0:T(2,128)S(1)} %get-tuple-element.40), channel_id=1, source_target_pairs={{1,0},{2,1},{3,2},{4,3},{5,4},{6,5},{7,6},{9,8},{10,9},{11,10},{12... | collective-permute-start | bytes 122888 | tf_op jit(solution)/shard_map/ppermute | solution.py:23
  193.7 27.8 %collective-permute-start.19 = (f32[2,20,2,128]{3,2,1,0:T(2,128)S(1)}, f32[2,20,2,128]{3,2,1,0:T(2,128)S(1)}, u32[]{:S(2)}, u32[]{:S(2)}) collective-permute-start(f32[2,20,2,128]{3,2,1,0:T(2,128)S(1)} %get-tuple-element.41), channel_id=1, source_target_pairs={{0,1},{1,2},{2,3},{3,4},{4,5},{5,6},{6,7},{8,9},{9,10},{10,11},{11... | collective-permute-start | bytes 122888 | tf_op jit(solution)/shard_map/ppermute | solution.py:21
  231.7 28.9 %collective-permute-start.22 = (f32[2,20,2,128]{3,2,1,0:T(2,128)S(1)}, f32[2,20,2,128]{3,2,1,0:T(2,128)S(1)}, u32[]{:S(2)}, u32[]{:S(2)}) collective-permute-start(f32[2,20,2,128]{3,2,1,0:T(2,128)S(1)} %get-tuple-element.36), channel_id=1, source_target_pairs={{1,0},{2,1},{3,2},{4,3},{5,4},{6,5},{7,6},{9,8},{10,9},{11,10},{12... | collective-permute-start | bytes 122888 | tf_op jit(solution)/shard_map/ppermute | solution.py:23
  233.0 27.6 %collective-permute-start.23 = (f32[2,20,2,128]{3,2,1,0:T(2,128)S(1)}, f32[2,20,2,128]{3,2,1,0:T(2,128)S(1)}, u32[]{:S(2)}, u32[]{:S(2)}) collective-permute-start(f32[2,20,2,128]{3,2,1,0:T(2,128)S(1)} %get-tuple-element.37), channel_id=1, source_target_pairs={{0,1},{1,2},{2,3},{3,4},{4,5},{5,6},{6,7},{8,9},{9,10},{10,11},{11... | collective-permute-start | bytes 122888 | tf_op jit(solution)/shard_map/ppermute | solution.py:21
  264.1 6.8 %collective-permute-start.25 = (f32[2,2,32,128]{3,2,1,0:T(8,128)S(1)}, f32[2,2,32,128]{3,2,1,0:T(8,128)S(1)}, u32[]{:S(2)}, u32[]{:S(2)}) collective-permute-start(f32[2,2,32,128]{3,2,1,0:T(8,128)S(1)} %get-tuple-element.69), channel_id=1, source_target_pairs={{0,8},{8,16},{16,24},{1,9},{9,17},{17,25},{2,10},{10,18},{18,26},{... | collective-permute-start | bytes 196616 | tf_op jit(solution)/shard_map/ppermute | solution.py:21
  270.9 28.9 %collective-permute-start.26 = (f32[2,20,2,128]{3,2,1,0:T(2,128)S(1)}, f32[2,20,2,128]{3,2,1,0:T(2,128)S(1)}, u32[]{:S(2)}, u32[]{:S(2)}) collective-permute-start(f32[2,20,2,128]{3,2,1,0:T(2,128)S(1)} %get-tuple-element.32), channel_id=1, source_target_pairs={{1,0},{2,1},{3,2},{4,3},{5,4},{6,5},{7,6},{9,8},{10,9},{11,10},{12... | collective-permute-start | bytes 122888 | tf_op jit(solution)/shard_map/ppermute | solution.py:23
  272.2 27.6 %collective-permute-start.27 = (f32[2,20,2,128]{3,2,1,0:T(2,128)S(1)}, f32[2,20,2,128]{3,2,1,0:T(2,128)S(1)}, u32[]{:S(2)}, u32[]{:S(2)}) collective-permute-start(f32[2,20,2,128]{3,2,1,0:T(2,128)S(1)} %get-tuple-element.33), channel_id=1, source_target_pairs={{0,1},{1,2},{2,3},{3,4},{4,5},{5,6},{6,7},{8,9},{9,10},{10,11},{11... | collective-permute-start | bytes 122888 | tf_op jit(solution)/shard_map/ppermute | solution.py:21
  310.0 29.1 %collective-permute-start.30 = (f32[2,20,2,128]{3,2,1,0:T(2,128)S(1)}, f32[2,20,2,128]{3,2,1,0:T(2,128)S(1)}, u32[]{:S(2)}, u32[]{:S(2)}) collective-permute-start(f32[2,20,2,128]{3,2,1,0:T(2,128)S(1)} %get-tuple-element.28), channel_id=1, source_target_pairs={{1,0},{2,1},{3,2},{4,3},{5,4},{6,5},{7,6},{9,8},{10,9},{11,10},{12... | collective-permute-start | bytes 122888 | tf_op jit(solution)/shard_map/ppermute | solution.py:23
  311.3 27.8 %collective-permute-start.31 = (f32[2,20,2,128]{3,2,1,0:T(2,128)S(1)}, f32[2,20,2,128]{3,2,1,0:T(2,128)S(1)}, u32[]{:S(2)}, u32[]{:S(2)}) collective-permute-start(f32[2,20,2,128]{3,2,1,0:T(2,128)S(1)} %get-tuple-element.29), channel_id=1, source_target_pairs={{0,1},{1,2},{2,3},{3,4},{4,5},{5,6},{6,7},{8,9},{9,10},{10,11},{11... | collective-permute-start | bytes 122888 | tf_op jit(solution)/shard_map/ppermute | solution.py:21
  (22 other events, 717.0 us)
Sparse Core Ops, SparseCore 0:
  9.7 52.3 all-gather.1
where the time goes:
time: 554 us; the launch traced here: 553 us
  blocking collectives  183 us (33%)
  local copies, waits for them, and re-layouts  177 us (32%)
  starting transfers between devices  113 us (20%)
  waiting for transfers between devices  39.1 us (7%)
  other arithmetic  24.3 us (4%)
  between operations  16 us (3%)
    psum x1, blocking collectives, local(): traces = lax.psum(jnp.stack(recorded, axis=-1), ('gx', 'gy'))  183 us
    div x8, local copies, waits for them, and re-layouts, advance(): (2.0 * middle - (1.0 - damp) * previous + coef * laplace(extended) + inje...  134 us
    ppermute x16, starting transfers between devices, extended_2(): lax.ppermute(tail, axis, [(i, (i + 1) % count) for i in range(ends)])  92.2 us
    all_gather x1, waiting for transfers between devices, local(): piece = lax.all_gather(model_tiles, ('shot', 'gx'), axis=0, tiled=True)  24.6 us
    gather x8, local copies, waits for them, and re-layouts, sample(): field[:, jnp.clip(local_x, 0, size_x - 1), jnp.clip(local_y, 0, size_y -...  23.6 us
    ppermute x16, starting transfers between devices, extended_2(): lax.ppermute(head, axis, [((i + 1) % count, i) for i in range(ends)])  20.7 us
    div x8, other arithmetic, advance(): (2.0 * middle - (1.0 - damp) * previous + coef * laplace(extended) + inje...  16.9 us
    slice x16, local copies, waits for them, and re-layouts, depth_ahead(): return jnp.concatenate([field[..., reach:], filler], axis=-1)  12.5 us
  transfers between devices with their start and end apart: 33, of which 17 were waited for; matrix products, arithmetic and copies ran while one was open for 29% of the time, Pallas kernels for 0%

commit v1 on v0

--- a/solution.py
+++ b/solution.py
@@ -135,7 +135,7 @@
         recorded.append(sample(fresh, receiver_cells, x_start, y_start))
         previous = current
         current = fresh
-    traces = lax.psum(jnp.stack(recorded, axis=-1), ("gx", "gy"))
+    traces = lax.psum(lax.psum(jnp.stack(recorded, axis=-1), "gx"), "gy")
     return (current[None], previous[None], traces[None])
 
 

time: 554 us -> 432 us (0.78)
  blocking collectives: 183 us -> 60.9 us
    psum x1 -> x2, blocking collectives: 183 us -> 60.9 us  [local(): traces = lax.psum(lax.psum(jnp.stack(recorded, axis=-1), 'gx'), 'gy')]
  transfers between devices with their start and end apart: 33 -> 33, of which waited for: 17 -> 17; matrix products, arithmetic and copies ran while one was open for 29% -> 37% of each run, Pallas kernels for 0% -> 0%
where the time goes in v1:
time: 432 us; the launch traced here: 430 us
  local copies, waits for them, and re-layouts  177 us (41%)
  starting transfers between devices  113 us (26%)
  blocking collectives  60.9 us (14%)
  waiting for transfers between devices  39.1 us (9%)
  other arithmetic  24.3 us (6%)
  between operations  16 us (4%)
    div x8, local copies, waits for them, and re-layouts, advance(): (2.0 * middle - (1.0 - damp) * previous + coef * laplace(extended) + inje...  133 us
    ppermute x16, starting transfers between devices, extended_2(): lax.ppermute(tail, axis, [(i, (i + 1) % count) for i in range(ends)])  92.4 us
    psum x2, blocking collectives, local(): traces = lax.psum(lax.psum(jnp.stack(recorded, axis=-1), 'gx'), 'gy')  60.9 us
    all_gather x1, waiting for transfers between devices, local(): piece = lax.all_gather(model_tiles, ('shot', 'gx'), axis=0, tiled=True)  24.6 us
    gather x8, local copies, waits for them, and re-layouts, sample(): field[:, jnp.clip(local_x, 0, size_x - 1), jnp.clip(local_y, 0, size_y -...  23.6 us
    ppermute x16, starting transfers between devices, extended_2(): lax.ppermute(head, axis, [((i + 1) % count, i) for i in range(ends)])  20.7 us
    div x8, other arithmetic, advance(): (2.0 * middle - (1.0 - damp) * previous + coef * laplace(extended) + inje...  16.9 us
    slice x16, local copies, waits for them, and re-layouts, depth_ahead(): return jnp.concatenate([field[..., reach:], filler], axis=-1)  12.5 us
  transfers between devices with their start and end apart: 33, of which 17 were waited for; matrix products, arithmetic and copies ran while one was open for 37% of the time, Pallas kernels for 0%

profile of v1, /device:TPU:0, one launch (start us, length us, event | category | flops | bytes accessed | tf_op | source)
XLA Modules:
  0.0 430.3 jit_solution(9671258919910665084)
XLA Ops:
  28.2 6.1 %collective-permute-start.3 = (f32[2,20,2,128]{3,2,1,0:T(2,128)S(1)}, f32[2,20,2,128]{3,2,1,0:T(2,128)S(1)}, u32[]{:S(2)}, u32[]{:S(2)}) collective-permute-start(f32[2,20,2,128]{3,2,1,0:T(2,128)S(1)} %get-tuple-element.57), channel_id=1, source_target_pairs={{0,1},{1,2},{2,3},{3,4},{4,5},{5,6},{6,7},{8,9},{9,10},{10,11},{11... | collective-permute-start | bytes 122888 | tf_op jit(solution)/shard_map/ppermute | solution.py:21
  37.5 24.6 %all-gather.2.cloned.1.call-done = f32[256,32,128]{2,1,0:T(8,128)} async-done(((f32[16,32,128]{2,1,0:T(8,128)}), f32[256,32,128]{2,1,0:T(8,128)}) %all-gather.2.cloned.1.call-update) | async-done | bytes 4194320 | tf_op jit(solution)/shard_map/all_gather | solution.py:113
  77.4 6.1 %collective-permute-start.7 = (f32[2,20,2,128]{3,2,1,0:T(2,128)S(1)}, f32[2,20,2,128]{3,2,1,0:T(2,128)S(1)}, u32[]{:S(2)}, u32[]{:S(2)}) collective-permute-start(f32[2,20,2,128]{3,2,1,0:T(2,128)S(1)} %get-tuple-element.53), channel_id=1, source_target_pairs={{0,1},{1,2},{2,3},{3,4},{4,5},{5,6},{6,7},{8,9},{9,10},{10,11},{11... | collective-permute-start | bytes 122888 | tf_op jit(solution)/shard_map/ppermute | solution.py:21
  84.4 16.6 %copy.515 = f32[2,16,32,128]{0,3,2,1:T(8,128)} copy(f32[2,16,32,128]{3,2,1,0:T(8,128)S(1)} %fusion.94) | data formatting | bytes 1048576 | tf_op jit(solution)/shard_map/div | solution.py:86
  107.5 5.0 %collective-permute-start.9 = (f32[2,2,32,128]{3,2,1,0:T(8,128)S(1)}, f32[2,2,32,128]{3,2,1,0:T(8,128)S(1)}, u32[]{:S(2)}, u32[]{:S(2)}) collective-permute-start(f32[2,2,32,128]{3,2,1,0:T(8,128)S(1)} %get-tuple-element.93), channel_id=1, source_target_pairs={{0,8},{8,16},{16,24},{1,9},{9,17},{17,25},{2,10},{10,18},{18,26},{... | collective-permute-start | bytes 196616 | tf_op jit(solution)/shard_map/ppermute | solution.py:21
  115.8 6.5 %collective-permute-start.11 = (f32[2,20,2,128]{3,2,1,0:T(2,128)S(1)}, f32[2,20,2,128]{3,2,1,0:T(2,128)S(1)}, u32[]{:S(2)}, u32[]{:S(2)}) collective-permute-start(f32[2,20,2,128]{3,2,1,0:T(2,128)S(1)} %get-tuple-element.49), channel_id=1, source_target_pairs={{0,1},{1,2},{2,3},{3,4},{4,5},{5,6},{6,7},{8,9},{9,10},{10,11},{11... | collective-permute-start | bytes 122888 | tf_op jit(solution)/shard_map/ppermute | solution.py:21
  123.3 16.6 %copy.516 = f32[2,16,32,128]{0,3,2,1:T(8,128)} copy(f32[2,16,32,128]{3,2,1,0:T(8,128)S(1)} %fusion.82) | data formatting | bytes 1048576 | tf_op jit(solution)/shard_map/div | solution.py:86
  146.4 4.9 %collective-permute-start.13 = (f32[2,2,32,128]{3,2,1,0:T(8,128)S(1)}, f32[2,2,32,128]{3,2,1,0:T(8,128)S(1)}, u32[]{:S(2)}, u32[]{:S(2)}) collective-permute-start(f32[2,2,32,128]{3,2,1,0:T(8,128)S(1)} %get-tuple-element.87), channel_id=1, source_target_pairs={{0,8},{8,16},{16,24},{1,9},{9,17},{17,25},{2,10},{10,18},{18,26},{... | collective-permute-start | bytes 196616 | tf_op jit(solution)/shard_map/ppermute | solution.py:21
  154.5 7.0 %collective-permute-start.15 = (f32[2,20,2,128]{3,2,1,0:T(2,128)S(1)}, f32[2,20,2,128]{3,2,1,0:T(2,128)S(1)}, u32[]{:S(2)}, u32[]{:S(2)}) collective-permute-start(f32[2,20,2,128]{3,2,1,0:T(2,128)S(1)} %get-tuple-element.45), channel_id=1, source_target_pairs={{0,1},{1,2},{2,3},{3,4},{4,5},{5,6},{6,7},{8,9},{9,10},{10,11},{11... | collective-permute-start | bytes 122888 | tf_op jit(solution)/shard_map/ppermute | solution.py:21
  162.4 16.6 %copy.517 = f32[2,16,32,128]{0,3,2,1:T(8,128)} copy(f32[2,16,32,128]{3,2,1,0:T(8,128)S(1)} %fusion.70) | data formatting | bytes 1048576 | tf_op jit(solution)/shard_map/div | solution.py:86
  185.6 4.9 %collective-permute-start.17 = (f32[2,2,32,128]{3,2,1,0:T(8,128)S(1)}, f32[2,2,32,128]{3,2,1,0:T(8,128)S(1)}, u32[]{:S(2)}, u32[]{:S(2)}) collective-permute-start(f32[2,2,32,128]{3,2,1,0:T(8,128)S(1)} %get-tuple-element.81), channel_id=1, source_target_pairs={{0,8},{8,16},{16,24},{1,9},{9,17},{17,25},{2,10},{10,18},{18,26},{... | collective-permute-start | bytes 196616 | tf_op jit(solution)/shard_map/ppermute | solution.py:21
  193.7 7.1 %collective-permute-start.19 = (f32[2,20,2,128]{3,2,1,0:T(2,128)S(1)}, f32[2,20,2,128]{3,2,1,0:T(2,128)S(1)}, u32[]{:S(2)}, u32[]{:S(2)}) collective-permute-start(f32[2,20,2,128]{3,2,1,0:T(2,128)S(1)} %get-tuple-element.41), channel_id=1, source_target_pairs={{0,1},{1,2},{2,3},{3,4},{4,5},{5,6},{6,7},{8,9},{9,10},{10,11},{11... | collective-permute-start | bytes 122888 | tf_op jit(solution)/shard_map/ppermute | solution.py:21
  201.8 16.6 %copy.518 = f32[2,16,32,128]{0,3,2,1:T(8,128)} copy(f32[2,16,32,128]{3,2,1,0:T(8,128)S(1)} %fusion.58) | data formatting | bytes 1048576 | tf_op jit(solution)/shard_map/div | solution.py:86
  224.9 4.9 %collective-permute-start.21 = (f32[2,2,32,128]{3,2,1,0:T(8,128)S(1)}, f32[2,2,32,128]{3,2,1,0:T(8,128)S(1)}, u32[]{:S(2)}, u32[]{:S(2)}) collective-permute-start(f32[2,2,32,128]{3,2,1,0:T(8,128)S(1)} %get-tuple-element.75), channel_id=1, source_target_pairs={{0,8},{8,16},{16,24},{1,9},{9,17},{17,25},{2,10},{10,18},{18,26},{... | collective-permute-start | bytes 196616 | tf_op jit(solution)/shard_map/ppermute | solution.py:21
  233.0 7.0 %collective-permute-start.23 = (f32[2,20,2,128]{3,2,1,0:T(2,128)S(1)}, f32[2,20,2,128]{3,2,1,0:T(2,128)S(1)}, u32[]{:S(2)}, u32[]{:S(2)}) collective-permute-start(f32[2,20,2,128]{3,2,1,0:T(2,128)S(1)} %get-tuple-element.37), channel_id=1, source_target_pairs={{0,1},{1,2},{2,3},{3,4},{4,5},{5,6},{6,7},{8,9},{9,10},{10,11},{11... | collective-permute-start | bytes 122888 | tf_op jit(solution)/shard_map/ppermute | solution.py:21
  240.9 16.6 %copy.519 = f32[2,16,32,128]{0,3,2,1:T(8,128)} copy(f32[2,16,32,128]{3,2,1,0:T(8,128)S(1)} %fusion.46) | data formatting | bytes 1048576 | tf_op jit(solution)/shard_map/div | solution.py:86
  264.1 4.9 %collective-permute-start.25 = (f32[2,2,32,128]{3,2,1,0:T(8,128)S(1)}, f32[2,2,32,128]{3,2,1,0:T(8,128)S(1)}, u32[]{:S(2)}, u32[]{:S(2)}) collective-permute-start(f32[2,2,32,128]{3,2,1,0:T(8,128)S(1)} %get-tuple-element.69), channel_id=1, source_target_pairs={{0,8},{8,16},{16,24},{1,9},{9,17},{17,25},{2,10},{10,18},{18,26},{... | collective-permute-start | bytes 196616 | tf_op jit(solution)/shard_map/ppermute | solution.py:21
  272.2 7.0 %collective-permute-start.27 = (f32[2,20,2,128]{3,2,1,0:T(2,128)S(1)}, f32[2,20,2,128]{3,2,1,0:T(2,128)S(1)}, u32[]{:S(2)}, u32[]{:S(2)}) collective-permute-start(f32[2,20,2,128]{3,2,1,0:T(2,128)S(1)} %get-tuple-element.33), channel_id=1, source_target_pairs={{0,1},{1,2},{2,3},{3,4},{4,5},{5,6},{6,7},{8,9},{9,10},{10,11},{11... | collective-permute-start | bytes 122888 | tf_op jit(solution)/shard_map/ppermute | solution.py:21
  280.1 16.6 %copy.520 = f32[2,16,32,128]{0,3,2,1:T(8,128)} copy(f32[2,16,32,128]{3,2,1,0:T(8,128)S(1)} %fusion.34) | data formatting | bytes 1048576 | tf_op jit(solution)/shard_map/div | solution.py:86
  311.4 7.2 %collective-permute-start.31 = (f32[2,20,2,128]{3,2,1,0:T(2,128)S(1)}, f32[2,20,2,128]{3,2,1,0:T(2,128)S(1)}, u32[]{:S(2)}, u32[]{:S(2)}) collective-permute-start(f32[2,20,2,128]{3,2,1,0:T(2,128)S(1)} %get-tuple-element.29), channel_id=1, source_target_pairs={{0,1},{1,2},{2,3},{3,4},{4,5},{5,6},{6,7},{8,9},{9,10},{10,11},{11... | collective-permute-start | bytes 122888 | tf_op jit(solution)/shard_map/ppermute | solution.py:21
  319.5 16.6 %copy.521 = f32[2,16,32,128]{0,3,2,1:T(8,128)} copy(f32[2,16,32,128]{3,2,1,0:T(8,128)S(1)} %fusion.22) | data formatting | bytes 1048576 | tf_op jit(solution)/shard_map/div | solution.py:86
  341.4 16.7 %copy.522 = f32[2,16,32,128]{0,3,2,1:T(8,128)} copy(f32[2,16,32,128]{3,2,1,0:T(8,128)S(1)} %fusion.10) | data formatting | bytes 1048576 | tf_op jit(solution)/shard_map/div | solution.py:86
  362.6 19.1 %psum.14 = f32[2,256,8]{1,2,0:T(8,128)S(1)} all-reduce(f32[2,256,8]{1,2,0:T(8,128)S(1)} %stack.2), channel_id=1, replica_groups=mesh['shot'=4,'gx'=4,'gy'=8] {'gx'}, use_global_device_ids=true, to_apply=%region_1.2 | all-reduce | flops 4096 | bytes 32768 | tf_op jit(solution)/shard_map/psum | solution.py:138
  381.7 41.8 %psum.15 = f32[1,2,256,8]{2,3,1,0:T(8,128)} all-reduce(f32[1,2,256,8]{2,3,1,0:T(8,128)S(1)} %bitcast.70), channel_id=1, replica_groups=mesh['shot'=4,'gx'=4,'gy'=8] {'gy'}, use_global_device_ids=true, to_apply=%region_2.3 | all-reduce | flops 4096 | bytes 32768 | tf_op jit(solution)/shard_map/psum | solution.py:138
  (165 shorter events, 117.2 us)
Async XLA Ops:
  7.2 54.9 %all-gather.2.cloned.1.call-start = ((), (), s32[]{:S(2)}) async-start(), calls=%async_computation | async-start | bytes 4456448 | tf_op jit(solution)/shard_map/all_gather | solution.py:113
  8.8 17.0 %collective-permute-start = (f32[2,2,32,128]{3,2,1,0:T(8,128)S(1)}, f32[2,2,32,128]{3,2,1,0:T(8,128)S(1)}, u32[]{:S(2)}, u32[]{:S(2)}) collective-permute-start(f32[2,2,32,128]{3,2,1,0:T(8,128)S(1)} %get-tuple-element.104), channel_id=1, source_target_pairs={{8,0},{16,8},{24,16},{9,1},{17,9},{25,17},{10,2},{18,10},{26,18},{... | collective-permute-start | bytes 196616 | tf_op jit(solution)/shard_map/ppermute | solution.py:23
  10.1 15.8 %collective-permute-start.1 = (f32[2,2,32,128]{3,2,1,0:T(8,128)S(1)}, f32[2,2,32,128]{3,2,1,0:T(8,128)S(1)}, u32[]{:S(2)}, u32[]{:S(2)}) collective-permute-start(f32[2,2,32,128]{3,2,1,0:T(8,128)S(1)} %get-tuple-element.105), channel_id=1, source_target_pairs={{0,8},{8,16},{16,24},{1,9},{9,17},{17,25},{2,10},{10,18},{18,26},{... | collective-permute-start | bytes 196616 | tf_op jit(solution)/shard_map/ppermute | solution.py:21
  26.9 7.7 %collective-permute-start.2 = (f32[2,20,2,128]{3,2,1,0:T(2,128)S(1)}, f32[2,20,2,128]{3,2,1,0:T(2,128)S(1)}, u32[]{:S(2)}, u32[]{:S(2)}) collective-permute-start(f32[2,20,2,128]{3,2,1,0:T(2,128)S(1)} %get-tuple-element.56), channel_id=1, source_target_pairs={{1,0},{2,1},{3,2},{4,3},{5,4},{6,5},{7,6},{9,8},{10,9},{11,10},{12... | collective-permute-start | bytes 122888 | tf_op jit(solution)/shard_map/ppermute | solution.py:23
  28.2 7.9 %collective-permute-start.3 = (f32[2,20,2,128]{3,2,1,0:T(2,128)S(1)}, f32[2,20,2,128]{3,2,1,0:T(2,128)S(1)}, u32[]{:S(2)}, u32[]{:S(2)}) collective-permute-start(f32[2,20,2,128]{3,2,1,0:T(2,128)S(1)} %get-tuple-element.57), channel_id=1, source_target_pairs={{0,1},{1,2},{2,3},{3,4},{4,5},{5,6},{6,7},{8,9},{9,10},{10,11},{11... | collective-permute-start | bytes 122888 | tf_op jit(solution)/shard_map/ppermute | solution.py:21
  76.1 28.0 %collective-permute-start.6 = (f32[2,20,2,128]{3,2,1,0:T(2,128)S(1)}, f32[2,20,2,128]{3,2,1,0:T(2,128)S(1)}, u32[]{:S(2)}, u32[]{:S(2)}) collective-permute-start(f32[2,20,2,128]{3,2,1,0:T(2,128)S(1)} %get-tuple-element.52), channel_id=1, source_target_pairs={{1,0},{2,1},{3,2},{4,3},{5,4},{6,5},{7,6},{9,8},{10,9},{11,10},{12... | collective-permute-start | bytes 122888 | tf_op jit(solution)/shard_map/ppermute | solution.py:23
  77.4 26.7 %collective-permute-start.7 = (f32[2,20,2,128]{3,2,1,0:T(2,128)S(1)}, f32[2,20,2,128]{3,2,1,0:T(2,128)S(1)}, u32[]{:S(2)}, u32[]{:S(2)}) collective-permute-start(f32[2,20,2,128]{3,2,1,0:T(2,128)S(1)} %get-tuple-element.53), channel_id=1, source_target_pairs={{0,1},{1,2},{2,3},{3,4},{4,5},{5,6},{6,7},{8,9},{9,10},{10,11},{11... | collective-permute-start | bytes 122888 | tf_op jit(solution)/shard_map/ppermute | solution.py:21
  107.5 6.9 %collective-permute-start.9 = (f32[2,2,32,128]{3,2,1,0:T(8,128)S(1)}, f32[2,2,32,128]{3,2,1,0:T(8,128)S(1)}, u32[]{:S(2)}, u32[]{:S(2)}) collective-permute-start(f32[2,2,32,128]{3,2,1,0:T(8,128)S(1)} %get-tuple-element.93), channel_id=1, source_target_pairs={{0,8},{8,16},{16,24},{1,9},{9,17},{17,25},{2,10},{10,18},{18,26},{... | collective-permute-start | bytes 196616 | tf_op jit(solution)/shard_map/ppermute | solution.py:21
  114.5 28.4 %collective-permute-start.10 = (f32[2,20,2,128]{3,2,1,0:T(2,128)S(1)}, f32[2,20,2,128]{3,2,1,0:T(2,128)S(1)}, u32[]{:S(2)}, u32[]{:S(2)}) collective-permute-start(f32[2,20,2,128]{3,2,1,0:T(2,128)S(1)} %get-tuple-element.48), channel_id=1, source_target_pairs={{1,0},{2,1},{3,2},{4,3},{5,4},{6,5},{7,6},{9,8},{10,9},{11,10},{12... | collective-permute-start | bytes 122888 | tf_op jit(solution)/shard_map/ppermute | solution.py:23
  115.8 27.1 %collective-permute-start.11 = (f32[2,20,2,128]{3,2,1,0:T(2,128)S(1)}, f32[2,20,2,128]{3,2,1,0:T(2,128)S(1)}, u32[]{:S(2)}, u32[]{:S(2)}) collective-permute-start(f32[2,20,2,128]{3,2,1,0:T(2,128)S(1)} %get-tuple-element.49), channel_id=1, source_target_pairs={{0,1},{1,2},{2,3},{3,4},{4,5},{5,6},{6,7},{8,9},{9,10},{10,11},{11... | collective-permute-start | bytes 122888 | tf_op jit(solution)/shard_map/ppermute | solution.py:21
  153.2 28.9 %collective-permute-start.14 = (f32[2,20,2,128]{3,2,1,0:T(2,128)S(1)}, f32[2,20,2,128]{3,2,1,0:T(2,128)S(1)}, u32[]{:S(2)}, u32[]{:S(2)}) collective-permute-start(f32[2,20,2,128]{3,2,1,0:T(2,128)S(1)} %get-tuple-element.44), channel_id=1, source_target_pairs={{1,0},{2,1},{3,2},{4,3},{5,4},{6,5},{7,6},{9,8},{10,9},{11,10},{12... | collective-permute-start | bytes 122888 | tf_op jit(solution)/shard_map/ppermute | solution.py:23
  154.5 27.6 %collective-permute-start.15 = (f32[2,20,2,128]{3,2,1,0:T(2,128)S(1)}, f32[2,20,2,128]{3,2,1,0:T(2,128)S(1)}, u32[]{:S(2)}, u32[]{:S(2)}) collective-permute-start(f32[2,20,2,128]{3,2,1,0:T(2,128)S(1)} %get-tuple-element.45), channel_id=1, source_target_pairs={{0,1},{1,2},{2,3},{3,4},{4,5},{5,6},{6,7},{8,9},{9,10},{10,11},{11... | collective-permute-start | bytes 122888 | tf_op jit(solution)/shard_map/ppermute | solution.py:21
  185.6 6.8 %collective-permute-start.17 = (f32[2,2,32,128]{3,2,1,0:T(8,128)S(1)}, f32[2,2,32,128]{3,2,1,0:T(8,128)S(1)}, u32[]{:S(2)}, u32[]{:S(2)}) collective-permute-start(f32[2,2,32,128]{3,2,1,0:T(8,128)S(1)} %get-tuple-element.81), channel_id=1, source_target_pairs={{0,8},{8,16},{16,24},{1,9},{9,17},{17,25},{2,10},{10,18},{18,26},{... | collective-permute-start | bytes 196616 | tf_op jit(solution)/shard_map/ppermute | solution.py:21
  192.4 29.1 %collective-permute-start.18 = (f32[2,20,2,128]{3,2,1,0:T(2,128)S(1)}, f32[2,20,2,128]{3,2,1,0:T(2,128)S(1)}, u32[]{:S(2)}, u32[]{:S(2)}) collective-permute-start(f32[2,20,2,128]{3,2,1,0:T(2,128)S(1)} %get-tuple-element.40), channel_id=1, source_target_pairs={{1,0},{2,1},{3,2},{4,3},{5,4},{6,5},{7,6},{9,8},{10,9},{11,10},{12... | collective-permute-start | bytes 122888 | tf_op jit(solution)/shard_map/ppermute | solution.py:23
  193.7 27.8 %collective-permute-start.19 = (f32[2,20,2,128]{3,2,1,0:T(2,128)S(1)}, f32[2,20,2,128]{3,2,1,0:T(2,128)S(1)}, u32[]{:S(2)}, u32[]{:S(2)}) collective-permute-start(f32[2,20,2,128]{3,2,1,0:T(2,128)S(1)} %get-tuple-element.41), channel_id=1, source_target_pairs={{0,1},{1,2},{2,3},{3,4},{4,5},{5,6},{6,7},{8,9},{9,10},{10,11},{11... | collective-permute-start | bytes 122888 | tf_op jit(solution)/shard_map/ppermute | solution.py:21
  224.9 6.8 %collective-permute-start.21 = (f32[2,2,32,128]{3,2,1,0:T(8,128)S(1)}, f32[2,2,32,128]{3,2,1,0:T(8,128)S(1)}, u32[]{:S(2)}, u32[]{:S(2)}) collective-permute-start(f32[2,2,32,128]{3,2,1,0:T(8,128)S(1)} %get-tuple-element.75), channel_id=1, source_target_pairs={{0,8},{8,16},{16,24},{1,9},{9,17},{17,25},{2,10},{10,18},{18,26},{... | collective-permute-start | bytes 196616 | tf_op jit(solution)/shard_map/ppermute | solution.py:21
  231.7 28.9 %collective-permute-start.22 = (f32[2,20,2,128]{3,2,1,0:T(2,128)S(1)}, f32[2,20,2,128]{3,2,1,0:T(2,128)S(1)}, u32[]{:S(2)}, u32[]{:S(2)}) collective-permute-start(f32[2,20,2,128]{3,2,1,0:T(2,128)S(1)} %get-tuple-element.36), channel_id=1, source_target_pairs={{1,0},{2,1},{3,2},{4,3},{5,4},{6,5},{7,6},{9,8},{10,9},{11,10},{12... | collective-permute-start | bytes 122888 | tf_op jit(solution)/shard_map/ppermute | solution.py:23
  233.0 27.6 %collective-permute-start.23 = (f32[2,20,2,128]{3,2,1,0:T(2,128)S(1)}, f32[2,20,2,128]{3,2,1,0:T(2,128)S(1)}, u32[]{:S(2)}, u32[]{:S(2)}) collective-permute-start(f32[2,20,2,128]{3,2,1,0:T(2,128)S(1)} %get-tuple-element.37), channel_id=1, source_target_pairs={{0,1},{1,2},{2,3},{3,4},{4,5},{5,6},{6,7},{8,9},{9,10},{10,11},{11... | collective-permute-start | bytes 122888 | tf_op jit(solution)/shard_map/ppermute | solution.py:21
  264.1 6.8 %collective-permute-start.25 = (f32[2,2,32,128]{3,2,1,0:T(8,128)S(1)}, f32[2,2,32,128]{3,2,1,0:T(8,128)S(1)}, u32[]{:S(2)}, u32[]{:S(2)}) collective-permute-start(f32[2,2,32,128]{3,2,1,0:T(8,128)S(1)} %get-tuple-element.69), channel_id=1, source_target_pairs={{0,8},{8,16},{16,24},{1,9},{9,17},{17,25},{2,10},{10,18},{18,26},{... | collective-permute-start | bytes 196616 | tf_op jit(solution)/shard_map/ppermute | solution.py:21
  270.9 28.9 %collective-permute-start.26 = (f32[2,20,2,128]{3,2,1,0:T(2,128)S(1)}, f32[2,20,2,128]{3,2,1,0:T(2,128)S(1)}, u32[]{:S(2)}, u32[]{:S(2)}) collective-permute-start(f32[2,20,2,128]{3,2,1,0:T(2,128)S(1)} %get-tuple-element.32), channel_id=1, source_target_pairs={{1,0},{2,1},{3,2},{4,3},{5,4},{6,5},{7,6},{9,8},{10,9},{11,10},{12... | collective-permute-start | bytes 122888 | tf_op jit(solution)/shard_map/ppermute | solution.py:23
  272.2 27.6 %collective-permute-start.27 = (f32[2,20,2,128]{3,2,1,0:T(2,128)S(1)}, f32[2,20,2,128]{3,2,1,0:T(2,128)S(1)}, u32[]{:S(2)}, u32[]{:S(2)}) collective-permute-start(f32[2,20,2,128]{3,2,1,0:T(2,128)S(1)} %get-tuple-element.33), channel_id=1, source_target_pairs={{0,1},{1,2},{2,3},{3,4},{4,5},{5,6},{6,7},{8,9},{9,10},{10,11},{11... | collective-permute-start | bytes 122888 | tf_op jit(solution)/shard_map/ppermute | solution.py:21
  303.3 6.8 %collective-permute-start.29 = (f32[2,2,32,128]{3,2,1,0:T(8,128)S(1)}, f32[2,2,32,128]{3,2,1,0:T(8,128)S(1)}, u32[]{:S(2)}, u32[]{:S(2)}) collective-permute-start(f32[2,2,32,128]{3,2,1,0:T(8,128)S(1)} %get-tuple-element.63), channel_id=1, source_target_pairs={{0,8},{8,16},{16,24},{1,9},{9,17},{17,25},{2,10},{10,18},{18,26},{... | collective-permute-start | bytes 196616 | tf_op jit(solution)/shard_map/ppermute | solution.py:21
  310.1 29.1 %collective-permute-start.30 = (f32[2,20,2,128]{3,2,1,0:T(2,128)S(1)}, f32[2,20,2,128]{3,2,1,0:T(2,128)S(1)}, u32[]{:S(2)}, u32[]{:S(2)}) collective-permute-start(f32[2,20,2,128]{3,2,1,0:T(2,128)S(1)} %get-tuple-element.28), channel_id=1, source_target_pairs={{1,0},{2,1},{3,2},{4,3},{5,4},{6,5},{7,6},{9,8},{10,9},{11,10},{12... | collective-permute-start | bytes 122888 | tf_op jit(solution)/shard_map/ppermute | solution.py:23
  311.4 27.8 %collective-permute-start.31 = (f32[2,20,2,128]{3,2,1,0:T(2,128)S(1)}, f32[2,20,2,128]{3,2,1,0:T(2,128)S(1)}, u32[]{:S(2)}, u32[]{:S(2)}) collective-permute-start(f32[2,20,2,128]{3,2,1,0:T(2,128)S(1)} %get-tuple-element.29), channel_id=1, source_target_pairs={{0,1},{1,2},{2,3},{3,4},{4,5},{5,6},{6,7},{8,9},{9,10},{10,11},{11... | collective-permute-start | bytes 122888 | tf_op jit(solution)/shard_map/ppermute | solution.py:21
  (22 other events, 594.3 us)
Sparse Core Ops, SparseCore 0:
  9.7 52.3 all-gather.1
